TPU v7x, 256 devices: a whole 4x4x8 slice. The times are simulated.
256 devices in a mesh: freq: 8 (over y, z_hi), dom: 32 (over x, z_lo, core).
Axes of the slice: x: 4, y: 4, z: 8 (z_hi: 2, z_lo: 4; z = z_hi * 4 + z_lo), core: 2. Of those that a mesh axis runs over, the one named last changes fastest.
Arguments:
- fwd_source: float32 [16, 4, 1024, 128], P('freq', None, 'dom'), may hold values from -6 to 6
- adj_source: float32 [16, 4, 1024, 128], P('freq', None, 'dom'), may hold values from -6 to 6
- curl_blocks: float32 [1024, 4, 128, 128], P('dom')
- block_links: int32 [1024, 4], P('dom'), may hold values from 0 to 95, as said below
- tile_lists: int32 [128, 16], P('dom'), may hold values from 0 to 31, as said below
- edge_mass: float32 [1024, 128], P('dom'), may hold values from 0.5 to 1.5
- omega: float32 [16], P('freq'), may hold values from 0.1 to 1
- cell_edges: int32 [12, 32768], P(None, 'dom'), may hold values from 0 to 4095
- log_cond: float32 [32768], P('dom'), may hold values from -6 to 6
Outputs:
- fwd_field: float32 [16, 4, 1024, 128], P('freq', None, 'dom')
- adj_field: float32 [16, 4, 1024, 128], P('freq', None, 'dom')
- model_next: float32 [32768], P('dom')
Inputs may be any that keep to these rules, and one draw needn't show every extreme that they name: `block_links`: entry 0 of each block row is the row's own local block; the others index the partition's extended field, local blocks first, then the tiles received in round 0, 1 and so on; every received tile is referenced by some row of the partition. `tile_lists`: the 16 blocks of one row are distinct local blocks.
All inputs are finite; a program needn't handle non-finite values.
Results may differ from a plain program's by a relative error of at most 0.0001.
Values sent between devices are 32-bit elements; how exact they have to be, the bound alone decides.
No kernel may reach another device: no remote copies, remote signals or barrier semaphores. Data moves between devices by JAX's collectives and lax.ppermute only.
A program may use at most 64 MiB of HBM per device.

v0:
```python
import jax
import jax.numpy as jnp
from jax import lax
from jax.sharding import PartitionSpec as P

ITERS = 3


def swapped(value, axis, distance):
    mask = 2**distance
    pairs = [(source, source ^ mask) for source in range(lax.axis_size(axis))]
    return lax.ppermute(value, axis, pairs)


def operate(field, curl_blocks, block_links, tile_lists, weight, trade):
    parts = [field]
    for bit in range(tile_lists.shape[0]):
        outgoing = jnp.take(field, tile_lists[bit], axis=0)
        parts.append(trade(outgoing, bit))
    extended = jnp.concatenate(parts, axis=0)
    shape = field.shape
    gathered = jnp.take(extended, block_links.reshape(-1), axis=0)
    gathered = gathered.reshape(block_links.shape + shape[1:])
    curl = jnp.einsum("blij,blmj->bmi", curl_blocks, gathered, precision=lax.Precision.HIGHEST)
    count = weight.shape[2]
    curl = curl.reshape(shape[0], -1, count, 2, 2, shape[2])
    split = field.reshape(shape[0], -1, count, 2, 2, shape[2])
    real_part = curl[:, :, :, :, 0] - weight * split[:, :, :, :, 1]
    imag_part = curl[:, :, :, :, 1] + weight * split[:, :, :, :, 0]
    return jnp.stack([real_part, imag_part], axis=4).reshape(shape)


def chebyshev(source, curl_blocks, block_links, tile_lists, weight, trade):
    theta = 1.0
    delta = 0.7
    sone = theta / delta
    rho = 1.0 / sone
    solution = jnp.zeros_like(source)
    resid = source
    direction = source / theta
    for step in range(ITERS):
        solution = solution + direction
        if step + 1 < ITERS:
            resid = resid - operate(direction, curl_blocks, block_links, tile_lists, weight, trade)
            rho_new = 1.0 / (2.0 * sone - rho)
            direction = rho_new * rho * direction + 2.0 * rho_new / delta * resid
            rho = rho_new
    return solution


def to_rows(fields):
    shape = fields.shape
    moved = jnp.transpose(fields, (3, 0, 1, 2, 4))
    return moved.reshape(shape[3], shape[0] * shape[1] * shape[2], shape[4])


def from_rows(rows, systems, count):
    shaped = rows.reshape(rows.shape[0], systems, count, 4, rows.shape[2])
    return jnp.transpose(shaped, (1, 2, 3, 0, 4))


def local(
    fwd_source,
    adj_source,
    curl_blocks,
    block_links,
    tile_lists,
    edge_mass,
    omega,
    cell_edges,
    log_cond,
):
    count = fwd_source.shape[0]
    weight = (edge_mass[:, None, :] * omega[None, :, None])[:, None, :, None, :]

    def trade_one(outgoing, bit):
        return swapped(outgoing, "dom", bit)

    fwd_rows = chebyshev(
        to_rows(fwd_source[None]), curl_blocks, block_links, tile_lists, weight, trade_one
    )
    adj_rows = chebyshev(
        to_rows(adj_source[None]), curl_blocks, block_links, tile_lists, weight, trade_one
    )
    efield = from_rows(fwd_rows, 1, count)[0]
    lfield = from_rows(adj_rows, 1, count)[0]
    edges = efield.shape[2] * efield.shape[3]
    esplit = efield.reshape(count, 2, 2, edges)
    lsplit = lfield.reshape(count, 2, 2, edges)
    prod = esplit[:, :, 0] * lsplit[:, :, 1] + esplit[:, :, 1] * lsplit[:, :, 0]
    edge_term = jnp.sum(omega[:, None, None] * prod, axis=(0, 1))
    picked = jnp.take(edge_term, cell_edges.reshape(-1), axis=0).reshape(cell_edges.shape)
    scale = 1.0 / jnp.sqrt(24.0 * count * lax.axis_size("freq"))
    partial_grad = jnp.sum(picked, axis=0) * scale
    grad = lax.psum(partial_grad, "freq")
    model_next = log_cond - 0.5 * grad / jnp.sqrt(grad * grad + 1.0)
    return (efield, lfield, model_next)


def solution(mesh):
    in_specs = (
        P("freq", None, "dom", None),
        P("freq", None, "dom", None),
        P("dom", None, None, None),
        P("dom", None),
        P("dom", None),
        P("dom", None),
        P("freq"),
        P(None, "dom"),
        P("dom"),
    )
    out_specs = (P("freq", None, "dom", None), P("freq", None, "dom", None), P("dom"))
    return jax.shard_map(local, mesh=mesh, in_specs=in_specs, out_specs=out_specs, check_vma=False)
```

profile of v0, /device:TPU:4, one launch (start us, length us, event | category | flops | bytes accessed | tf_op | source)
XLA Modules:
  0.0 182.5 jit_solution(15824569040240050575)
XLA Ops:
  0.6 0.8 compare_and_fusion.1
  1.5 1.0 copy.47
  2.5 1.0 copy.51
  3.5 0.6 gather_fusion.1
  4.1 0.6 gather_fusion.11
  4.6 0.1 broadcast_select_fusion.11
  4.7 0.1 collective-permute-start
  4.8 0.6 gather_fusion.2
  5.4 0.6 gather_fusion.12
  6.1 2.0 %collective-permute-start.1 = (f32[16,8,128]{2,1,0:T(8,128)S(1)}, f32[16,8,128]{2,1,0:T(8,128)S(1)}, u32[]{:S(2)}, u32[]{:S(2)}) collective-permute-start(f32[16,8,128]{2,1,0:T(8,128)S(1)} %get-tuple-element.60), channel_id=1, source_target_pairs={{0,2},{1,3},{2,0},{3,1},{4,6},{5,7},{6,4},{7,5},{8,10},{9,11},{10,... | collective-permute-start | bytes 196616 | tf_op jit(solution)/shard_map/ppermute | solution.py:12
  8.1 0.6 gather_fusion.3
  8.7 0.6 gather_fusion.13
  9.3 3.4 %collective-permute-start.2 = (f32[16,8,128]{2,1,0:T(8,128)S(1)}, f32[16,8,128]{2,1,0:T(8,128)S(1)}, u32[]{:S(2)}, u32[]{:S(2)}) collective-permute-start(f32[16,8,128]{2,1,0:T(8,128)S(1)} %get-tuple-element.58), channel_id=1, source_target_pairs={{0,4},{1,5},{2,6},{3,7},{4,0},{5,1},{6,2},{7,3},{8,12},{9,13},{10,... | collective-permute-start | bytes 196616 | tf_op jit(solution)/shard_map/ppermute | solution.py:12
  12.7 0.6 gather_fusion.4
  13.3 0.6 gather_fusion.14
  13.8 0.1 broadcast_select_fusion.8
  13.9 1.3 collective-permute-start.3
  15.2 0.8 copy.46
  16.0 0.1 reshape.267
  16.1 0.9 copy.60
  17.1 0.8 broadcast_multiply_fusion
  17.9 0.2 collective-permute-start.9
  18.1 0.3 collective-permute-start.10
  18.4 1.1 collective-permute-start.11
  19.5 0.8 gather_fusion.5
  20.3 3.4 %collective-permute-done.9 = f32[16,8,128]{2,1,0:T(8,128)S(1)} collective-permute-done((f32[16,8,128]{2,1,0:T(8,128)S(1)}, f32[16,8,128]{2,1,0:T(8,128)S(1)}, u32[]{:S(2)}, u32[]{:S(2)}) %collective-permute-start.9) | collective-permute-done | bytes 65568 | tf_op jit(solution)/shard_map/ppermute | solution.py:12
  23.7 1.3 collective-permute-done.10
  25.0 0.8 gather_fusion.15
  25.8 0.2 broadcast_select_fusion.1
  26.0 9.3 %convolution_bitcast_fusion.3 = f32[32,8,128]{2,1,0:T(8,128)S(1)} fusion(f32[32,4,8,128]{3,2,1,0:T(8,128)S(1)} %bitcast.106, f32[32,4,128,128]{3,2,1,0:T(8,128)} %param.15), kind=kOutput, calls=%fused_computation.24 | convolution fusion | flops 201326592 | bytes 9043968 | tf_op jit(solution)/shard_map/blij,blmj->bmi/dot_general | solution.py:24
  35.4 9.3 %convolution_bitcast_fusion.1 = f32[32,8,128]{2,1,0:T(8,128)S(1)} fusion(f32[32,4,8,128]{3,2,1,0:T(8,128)S(1)} %bitcast.104, f32[32,4,128,128]{3,2,1,0:T(8,128)} %param.15), kind=kOutput, calls=%fused_computation.22 | convolution fusion | flops 201326592 | bytes 9043968 | tf_op jit(solution)/shard_map/blij,blmj->bmi/dot_general | solution.py:24
  44.8 0.1 constant_dynamic-update-slice_fusion.9
  44.9 0.6 gather_fusion.6
  45.5 0.6 gather_fusion.7
  46.1 0.1 constant_dynamic-update-slice_fusion.19
  46.2 0.6 gather_fusion.16
  46.8 0.6 gather_fusion.17
  47.3 0.6 gather_fusion.8
  47.9 0.6 gather_fusion.18
  48.5 0.6 gather_fusion.9
  49.1 0.6 gather_fusion.19
  49.6 0.1 broadcast_select_fusion.7
  49.7 0.1 collective-permute-start.4
  49.9 0.4 collective-permute-start.5
  50.4 2.3 %collective-permute-start.6 = (f32[16,8,128]{2,1,0:T(8,128)S(1)}, f32[16,8,128]{2,1,0:T(8,128)S(1)}, u32[]{:S(2)}, u32[]{:S(2)}) collective-permute-start(f32[16,8,128]{2,1,0:T(8,128)S(1)} %get-tuple-element.48), channel_id=1, source_target_pairs={{0,4},{1,5},{2,6},{3,7},{4,0},{5,1},{6,2},{7,3},{8,12},{9,13},{10,... | collective-permute-start | bytes 196616 | tf_op jit(solution)/shard_map/ppermute | solution.py:12
  52.8 0.9 collective-permute-start.7
  53.8 1.2 collective-permute-start.15
  55.0 0.7 collective-permute-start.14
  55.7 1.8 collective-permute-start.13
  57.4 0.3 collective-permute-start.12
  57.8 0.8 gather_fusion.10
  58.6 0.4 collective-permute-done.12
  59.0 1.7 collective-permute-done.13
  60.8 0.8 gather_fusion.20
  61.6 0.2 broadcast_select_fusion
  61.8 9.3 %convolution_bitcast_fusion.2 = f32[32,8,128]{2,1,0:T(8,128)S(1)} fusion(f32[32,4,8,128]{3,2,1,0:T(8,128)S(1)} %bitcast.105, f32[32,4,128,128]{3,2,1,0:T(8,128)} %param.15), kind=kOutput, calls=%fused_computation.23 | convolution fusion | flops 201326592 | bytes 9043968 | tf_op jit(solution)/shard_map/blij,blmj->bmi/dot_general | solution.py:24
  71.1 9.3 %convolution_bitcast_fusion = f32[32,8,128]{2,1,0:T(8,128)S(1)} fusion(f32[32,4,8,128]{3,2,1,0:T(8,128)S(1)} %bitcast.103, f32[32,4,128,128]{3,2,1,0:T(8,128)} %param.15), kind=kOutput, calls=%fused_computation.21 | convolution fusion | flops 201326592 | bytes 9043968 | tf_op jit(solution)/shard_map/blij,blmj->bmi/dot_general | solution.py:24
  80.4 0.7 fusion.17
  81.2 0.7 fusion.15
  82.0 0.1 fusion.4
  82.2 0.1 fusion.13
  82.3 68.0 %gather_fusion = f32[12288]{0:T(1024)S(1)} fusion(f32[4096]{0:T(1024)S(1)} %fusion.13, s32[12288]{0:T(1024)S(1)} %broadcast_clamp_fusion), kind=kCustom, calls=%fused_computation.20 | custom fusion | bytes 147456 | tf_op jit(solution)/shard_map/jit(_take)/gather | solution.py:92
  150.5 31.5 %psum.7 = f32[1024]{0:T(1024)S(1)} all-reduce(f32[1024]{0:T(1024)S(1)} %broadcast_multiply_fusion.1), channel_id=1, replica_groups=mesh['freq'=8,'dom'=32] {'freq'}, use_global_device_ids=true, to_apply=%region_2.5 | all-reduce | flops 1024 | bytes 8192 | tf_op jit(solution)/shard_map/psum | solution.py:95
  181.9 0.6 multiply_subtract_fusion
  (69 shorter events, 1.2 us)
Async XLA Ops:
  4.7 13.2 %collective-permute-start = (f32[16,8,128]{2,1,0:T(8,128)S(1)}, f32[16,8,128]{2,1,0:T(8,128)S(1)}, u32[]{:S(2)}, u32[]{:S(2)}) collective-permute-start(f32[16,8,128]{2,1,0:T(8,128)S(1)} %get-tuple-element.62), channel_id=1, source_target_pairs={{0,1},{1,0},{2,3},{3,2},{4,5},{5,4},{6,7},{7,6},{8,9},{9,8},{10,11... | collective-permute-start | bytes 196616 | tf_op jit(solution)/shard_map/ppermute | solution.py:12
  6.1 12.1 %collective-permute-start.1 = (f32[16,8,128]{2,1,0:T(8,128)S(1)}, f32[16,8,128]{2,1,0:T(8,128)S(1)}, u32[]{:S(2)}, u32[]{:S(2)}) collective-permute-start(f32[16,8,128]{2,1,0:T(8,128)S(1)} %get-tuple-element.60), channel_id=1, source_target_pairs={{0,2},{1,3},{2,0},{3,1},{4,6},{5,7},{6,4},{7,5},{8,10},{9,11},{10,... | collective-permute-start | bytes 196616 | tf_op jit(solution)/shard_map/ppermute | solution.py:12
  9.3 9.1 %collective-permute-start.2 = (f32[16,8,128]{2,1,0:T(8,128)S(1)}, f32[16,8,128]{2,1,0:T(8,128)S(1)}, u32[]{:S(2)}, u32[]{:S(2)}) collective-permute-start(f32[16,8,128]{2,1,0:T(8,128)S(1)} %get-tuple-element.58), channel_id=1, source_target_pairs={{0,4},{1,5},{2,6},{3,7},{4,0},{5,1},{6,2},{7,3},{8,12},{9,13},{10,... | collective-permute-start | bytes 196616 | tf_op jit(solution)/shard_map/ppermute | solution.py:12
  13.9 5.6 %collective-permute-start.3 = (f32[16,8,128]{2,1,0:T(8,128)S(1)}, f32[16,8,128]{2,1,0:T(8,128)S(1)}, u32[]{:S(2)}, u32[]{:S(2)}) collective-permute-start(f32[16,8,128]{2,1,0:T(8,128)S(1)} %get-tuple-element.56), channel_id=1, source_target_pairs={{0,8},{1,9},{2,10},{3,11},{4,12},{5,13},{6,14},{7,15},{8,0},{9,1},... | collective-permute-start | bytes 196616 | tf_op jit(solution)/shard_map/ppermute | solution.py:12
  15.2 5.1 %collective-permute-start.8 = (f32[16,8,128]{2,1,0:T(8,128)S(1)}, f32[16,8,128]{2,1,0:T(8,128)S(1)}, u32[]{:S(2)}, u32[]{:S(2)}) collective-permute-start(f32[16,8,128]{2,1,0:T(8,128)S(1)} %get-tuple-element.61), channel_id=1, source_target_pairs={{0,1},{1,0},{2,3},{3,2},{4,5},{5,4},{6,7},{7,6},{8,9},{9,8},{10,11... | collective-permute-start | bytes 196616 | tf_op jit(solution)/shard_map/ppermute | solution.py:12
  17.9 5.8 %collective-permute-start.9 = (f32[16,8,128]{2,1,0:T(8,128)S(1)}, f32[16,8,128]{2,1,0:T(8,128)S(1)}, u32[]{:S(2)}, u32[]{:S(2)}) collective-permute-start(f32[16,8,128]{2,1,0:T(8,128)S(1)} %get-tuple-element.59), channel_id=1, source_target_pairs={{0,2},{1,3},{2,0},{3,1},{4,6},{5,7},{6,4},{7,5},{8,10},{9,11},{10,... | collective-permute-start | bytes 196616 | tf_op jit(solution)/shard_map/ppermute | solution.py:12
  18.1 6.9 %collective-permute-start.10 = (f32[16,8,128]{2,1,0:T(8,128)S(1)}, f32[16,8,128]{2,1,0:T(8,128)S(1)}, u32[]{:S(2)}, u32[]{:S(2)}) collective-permute-start(f32[16,8,128]{2,1,0:T(8,128)S(1)} %get-tuple-element.57), channel_id=1, source_target_pairs={{0,4},{1,5},{2,6},{3,7},{4,0},{5,1},{6,2},{7,3},{8,12},{9,13},{10,... | collective-permute-start | bytes 196616 | tf_op jit(solution)/shard_map/ppermute | solution.py:12
  18.4 6.6 %collective-permute-start.11 = (f32[16,8,128]{2,1,0:T(8,128)S(1)}, f32[16,8,128]{2,1,0:T(8,128)S(1)}, u32[]{:S(2)}, u32[]{:S(2)}) collective-permute-start(f32[16,8,128]{2,1,0:T(8,128)S(1)} %get-tuple-element.55), channel_id=1, source_target_pairs={{0,8},{1,9},{2,10},{3,11},{4,12},{5,13},{6,14},{7,15},{8,0},{9,1},... | collective-permute-start | bytes 196616 | tf_op jit(solution)/shard_map/ppermute | solution.py:12
  26.0 18.7 %copy-start = (f32[2,4,32,128]{3,2,1,0:T(8,128)S(1)}, f32[2,4,32,128]{3,2,1,0:T(8,128)}, u32[]{:S(2)}) copy-start(f32[2,4,32,128]{3,2,1,0:T(8,128)} %param.14) | copy-start | bytes 393220
  26.0 18.7 %copy-start.1 = (f32[2,4,32,128]{3,2,1,0:T(8,128)S(1)}, f32[2,4,32,128]{3,2,1,0:T(8,128)}, u32[]{:S(2)}) copy-start(f32[2,4,32,128]{3,2,1,0:T(8,128)} %param.13) | copy-start | bytes 393220
  49.7 5.2 %collective-permute-start.4 = (f32[16,8,128]{2,1,0:T(8,128)S(1)}, f32[16,8,128]{2,1,0:T(8,128)S(1)}, u32[]{:S(2)}, u32[]{:S(2)}) collective-permute-start(f32[16,8,128]{2,1,0:T(8,128)S(1)} %get-tuple-element.52), channel_id=1, source_target_pairs={{0,1},{1,0},{2,3},{3,2},{4,5},{5,4},{6,7},{7,6},{8,9},{9,8},{10,11... | collective-permute-start | bytes 196616 | tf_op jit(solution)/shard_map/ppermute | solution.py:12
  49.9 5.8 %collective-permute-start.5 = (f32[16,8,128]{2,1,0:T(8,128)S(1)}, f32[16,8,128]{2,1,0:T(8,128)S(1)}, u32[]{:S(2)}, u32[]{:S(2)}) collective-permute-start(f32[16,8,128]{2,1,0:T(8,128)S(1)} %get-tuple-element.50), channel_id=1, source_target_pairs={{0,2},{1,3},{2,0},{3,1},{4,6},{5,7},{6,4},{7,5},{8,10},{9,11},{10,... | collective-permute-start | bytes 196616 | tf_op jit(solution)/shard_map/ppermute | solution.py:12
  50.4 7.0 %collective-permute-start.6 = (f32[16,8,128]{2,1,0:T(8,128)S(1)}, f32[16,8,128]{2,1,0:T(8,128)S(1)}, u32[]{:S(2)}, u32[]{:S(2)}) collective-permute-start(f32[16,8,128]{2,1,0:T(8,128)S(1)} %get-tuple-element.48), channel_id=1, source_target_pairs={{0,4},{1,5},{2,6},{3,7},{4,0},{5,1},{6,2},{7,3},{8,12},{9,13},{10,... | collective-permute-start | bytes 196616 | tf_op jit(solution)/shard_map/ppermute | solution.py:12
  52.8 4.9 %collective-permute-start.7 = (f32[16,8,128]{2,1,0:T(8,128)S(1)}, f32[16,8,128]{2,1,0:T(8,128)S(1)}, u32[]{:S(2)}, u32[]{:S(2)}) collective-permute-start(f32[16,8,128]{2,1,0:T(8,128)S(1)} %get-tuple-element.46), channel_id=1, source_target_pairs={{0,8},{1,9},{2,10},{3,11},{4,12},{5,13},{6,14},{7,15},{8,0},{9,1},... | collective-permute-start | bytes 196616 | tf_op jit(solution)/shard_map/ppermute | solution.py:12
  53.8 7.0 %collective-permute-start.15 = (f32[16,8,128]{2,1,0:T(8,128)S(1)}, f32[16,8,128]{2,1,0:T(8,128)S(1)}, u32[]{:S(2)}, u32[]{:S(2)}) collective-permute-start(f32[16,8,128]{2,1,0:T(8,128)S(1)} %get-tuple-element.45), channel_id=1, source_target_pairs={{0,8},{1,9},{2,10},{3,11},{4,12},{5,13},{6,14},{7,15},{8,0},{9,1},... | collective-permute-start | bytes 196616 | tf_op jit(solution)/shard_map/ppermute | solution.py:12
  55.0 5.8 %collective-permute-start.14 = (f32[16,8,128]{2,1,0:T(8,128)S(1)}, f32[16,8,128]{2,1,0:T(8,128)S(1)}, u32[]{:S(2)}, u32[]{:S(2)}) collective-permute-start(f32[16,8,128]{2,1,0:T(8,128)S(1)} %get-tuple-element.47), channel_id=1, source_target_pairs={{0,4},{1,5},{2,6},{3,7},{4,0},{5,1},{6,2},{7,3},{8,12},{9,13},{10,... | collective-permute-start | bytes 196616 | tf_op jit(solution)/shard_map/ppermute | solution.py:12
  55.7 5.1 %collective-permute-start.13 = (f32[16,8,128]{2,1,0:T(8,128)S(1)}, f32[16,8,128]{2,1,0:T(8,128)S(1)}, u32[]{:S(2)}, u32[]{:S(2)}) collective-permute-start(f32[16,8,128]{2,1,0:T(8,128)S(1)} %get-tuple-element.49), channel_id=1, source_target_pairs={{0,2},{1,3},{2,0},{3,1},{4,6},{5,7},{6,4},{7,5},{8,10},{9,11},{10,... | collective-permute-start | bytes 196616 | tf_op jit(solution)/shard_map/ppermute | solution.py:12
  57.4 1.6 collective-permute-start.12
  71.0 11.1 %copy-start.4 = (f32[2]{0:T(128)S(1)}, f32[2]{0:T(128)}, u32[]{:S(2)}) copy-start(f32[2]{0:T(128)} %param.19) | copy-start | bytes 28
  82.3 68.1 %copy-start.2 = (s32[12,1024]{1,0:T(8,128)S(1)}, s32[12,1024]{1,0:T(8,128)}, u32[]{:S(2)}) copy-start(s32[12,1024]{1,0:T(8,128)} %param.20) | copy-start | bytes 147460
  82.3 99.6 %copy-start.3 = (f32[1024]{0:T(1024)S(1)}, f32[1024]{0:T(1024)}, u32[]{:S(2)}) copy-start(f32[1024]{0:T(1024)} %param.21) | copy-start | bytes 12292
where the time goes:
time: 183 us
  local copies, waits for them, and re-layouts  84.3 us (46%)
  matrix products  37 us (20%)
  blocking collectives  31.5 us (17%)
  starting transfers between devices  16 us (9%)
  waiting for transfers between devices  6.85 us (4%)
  other arithmetic  5.52 us (3%)
    gather x2, local copies, waits for them, and re-layouts, local(): jnp.take(edge_term, cell_edges.reshape(-1), axis=0)  68 us
    dot_general x4, matrix products, operate(): jnp.einsum('blij,blmj->bmi', curl_blocks, gathered, precision=lax.Precisi...  37 us
    psum x1, blocking collectives, local(): grad = lax.psum(partial_grad, 'freq')  31.5 us
    ppermute x16, starting transfers between devices, swapped(): return lax.ppermute(value, axis, pairs)  16 us
    gather x16, local copies, waits for them, and re-layouts, operate(): outgoing = jnp.take(field, tile_lists[bit], axis=0)  9.04 us
    ppermute x16, waiting for transfers between devices, swapped(): return lax.ppermute(value, axis, pairs)  6.85 us
  transfers between devices with their start and end apart: 16, of which 4 were waited for; matrix products, arithmetic and copies ran while one was open for 4% of the time, Pallas kernels for 0%

commit v1 on v0

--- a/solution.py
+++ b/solution.py
@@ -92,7 +92,7 @@
     picked = jnp.take(edge_term, cell_edges.reshape(-1), axis=0).reshape(cell_edges.shape)
     scale = 1.0 / jnp.sqrt(24.0 * count * lax.axis_size("freq"))
     partial_grad = jnp.sum(picked, axis=0) * scale
-    grad = lax.psum(partial_grad, "freq")
+    grad = jnp.sum(lax.all_gather(partial_grad, "freq"), axis=0)
     model_next = log_cond - 0.5 * grad / jnp.sqrt(grad * grad + 1.0)
     return (efield, lfield, model_next)
 

time: 183 us -> 195 us (1.066)
  blocking collectives: 31.5 us -> 44.1 us
    all_gather x0 -> x1, blocking collectives: none -> 44.1 us  [local(): grad = jnp.sum(lax.all_gather(partial_grad, 'freq'), axis=0)]
    psum x1 -> x0, blocking collectives: 31.5 us -> none  [local(): grad = lax.psum(partial_grad, 'freq')]
where the time goes in v1:
time: 195 us
  local copies, waits for them, and re-layouts  84.3 us (43%)
  blocking collectives  44.1 us (23%)
  matrix products  37 us (19%)
  starting transfers between devices  16 us (8%)
  waiting for transfers between devices  6.85 us (4%)
  other arithmetic  5.54 us (3%)
    gather x2, local copies, waits for them, and re-layouts, local(): jnp.take(edge_term, cell_edges.reshape(-1), axis=0)  68 us
    all_gather x1, blocking collectives, local(): grad = jnp.sum(lax.all_gather(partial_grad, 'freq'), axis=0)  44.1 us
    dot_general x4, matrix products, operate(): jnp.einsum('blij,blmj->bmi', curl_blocks, gathered, precision=lax.Precisi...  37 us
    ppermute x16, starting transfers between devices, swapped(): return lax.ppermute(value, axis, pairs)  16 us
    gather x16, local copies, waits for them, and re-layouts, operate(): outgoing = jnp.take(field, tile_lists[bit], axis=0)  9.04 us
    ppermute x16, waiting for transfers between devices, swapped(): return lax.ppermute(value, axis, pairs)  6.85 us
  transfers between devices with their start and end apart: 16, of which 4 were waited for; matrix products, arithmetic and copies ran while one was open for 4% of the time, Pallas kernels for 0%

profile of v1, /device:TPU:4, one launch (start us, length us, event | category | flops | bytes accessed | tf_op | source)
XLA Modules:
  0.0 195.2 jit_solution(3155854951451693965)
XLA Ops:
  0.6 0.8 compare_and_fusion.1
  1.5 1.0 copy.77
  2.5 1.0 copy.81
  3.5 0.6 gather_fusion.1
  4.1 0.6 gather_fusion.11
  4.6 0.1 broadcast_select_fusion.11
  4.7 0.1 collective-permute-start
  4.8 0.6 gather_fusion.2
  5.4 0.6 gather_fusion.12
  6.1 2.0 %collective-permute-start.1 = (f32[16,8,128]{2,1,0:T(8,128)S(1)}, f32[16,8,128]{2,1,0:T(8,128)S(1)}, u32[]{:S(2)}, u32[]{:S(2)}) collective-permute-start(f32[16,8,128]{2,1,0:T(8,128)S(1)} %get-tuple-element.60), channel_id=1, source_target_pairs={{0,2},{1,3},{2,0},{3,1},{4,6},{5,7},{6,4},{7,5},{8,10},{9,11},{10,... | collective-permute-start | bytes 196616 | tf_op jit(solution)/shard_map/ppermute | solution.py:12
  8.1 0.6 gather_fusion.3
  8.7 0.6 gather_fusion.13
  9.3 3.4 %collective-permute-start.2 = (f32[16,8,128]{2,1,0:T(8,128)S(1)}, f32[16,8,128]{2,1,0:T(8,128)S(1)}, u32[]{:S(2)}, u32[]{:S(2)}) collective-permute-start(f32[16,8,128]{2,1,0:T(8,128)S(1)} %get-tuple-element.58), channel_id=1, source_target_pairs={{0,4},{1,5},{2,6},{3,7},{4,0},{5,1},{6,2},{7,3},{8,12},{9,13},{10,... | collective-permute-start | bytes 196616 | tf_op jit(solution)/shard_map/ppermute | solution.py:12
  12.7 0.6 gather_fusion.4
  13.3 0.6 gather_fusion.14
  13.8 0.1 broadcast_select_fusion.8
  13.9 1.3 collective-permute-start.3
  15.2 0.8 copy.76
  16.0 0.1 reshape.276
  16.1 0.9 copy.90
  17.1 0.8 broadcast_multiply_fusion
  17.9 0.2 collective-permute-start.9
  18.1 0.3 collective-permute-start.10
  18.4 1.1 collective-permute-start.11
  19.5 0.8 gather_fusion.5
  20.3 3.4 %collective-permute-done.9 = f32[16,8,128]{2,1,0:T(8,128)S(1)} collective-permute-done((f32[16,8,128]{2,1,0:T(8,128)S(1)}, f32[16,8,128]{2,1,0:T(8,128)S(1)}, u32[]{:S(2)}, u32[]{:S(2)}) %collective-permute-start.9) | collective-permute-done | bytes 65568 | tf_op jit(solution)/shard_map/ppermute | solution.py:12
  23.7 1.3 collective-permute-done.10
  25.0 0.8 gather_fusion.15
  25.8 0.2 broadcast_select_fusion.1
  26.0 9.3 %convolution_bitcast_fusion.3 = f32[32,8,128]{2,1,0:T(8,128)S(1)} fusion(f32[32,4,8,128]{3,2,1,0:T(8,128)S(1)} %bitcast.106, f32[32,4,128,128]{3,2,1,0:T(8,128)} %param.15), kind=kOutput, calls=%fused_computation.24 | convolution fusion | flops 201326592 | bytes 9043968 | tf_op jit(solution)/shard_map/blij,blmj->bmi/dot_general | solution.py:24
  35.4 9.3 %convolution_bitcast_fusion.1 = f32[32,8,128]{2,1,0:T(8,128)S(1)} fusion(f32[32,4,8,128]{3,2,1,0:T(8,128)S(1)} %bitcast.104, f32[32,4,128,128]{3,2,1,0:T(8,128)} %param.15), kind=kOutput, calls=%fused_computation.22 | convolution fusion | flops 201326592 | bytes 9043968 | tf_op jit(solution)/shard_map/blij,blmj->bmi/dot_general | solution.py:24
  44.8 0.1 constant_dynamic-update-slice_fusion.9
  44.9 0.6 gather_fusion.6
  45.5 0.6 gather_fusion.7
  46.1 0.1 constant_dynamic-update-slice_fusion.19
  46.2 0.6 gather_fusion.16
  46.8 0.6 gather_fusion.17
  47.3 0.6 gather_fusion.8
  47.9 0.6 gather_fusion.18
  48.5 0.6 gather_fusion.9
  49.1 0.6 gather_fusion.19
  49.6 0.1 broadcast_select_fusion.7
  49.7 0.1 collective-permute-start.4
  49.9 0.4 collective-permute-start.5
  50.4 2.3 %collective-permute-start.6 = (f32[16,8,128]{2,1,0:T(8,128)S(1)}, f32[16,8,128]{2,1,0:T(8,128)S(1)}, u32[]{:S(2)}, u32[]{:S(2)}) collective-permute-start(f32[16,8,128]{2,1,0:T(8,128)S(1)} %get-tuple-element.48), channel_id=1, source_target_pairs={{0,4},{1,5},{2,6},{3,7},{4,0},{5,1},{6,2},{7,3},{8,12},{9,13},{10,... | collective-permute-start | bytes 196616 | tf_op jit(solution)/shard_map/ppermute | solution.py:12
  52.8 0.9 collective-permute-start.7
  53.8 1.2 collective-permute-start.15
  55.0 0.7 collective-permute-start.14
  55.7 1.8 collective-permute-start.13
  57.4 0.3 collective-permute-start.12
  57.8 0.8 gather_fusion.10
  58.6 0.4 collective-permute-done.12
  59.0 1.7 collective-permute-done.13
  60.8 0.8 gather_fusion.20
  61.6 0.2 broadcast_select_fusion
  61.8 9.3 %convolution_bitcast_fusion.2 = f32[32,8,128]{2,1,0:T(8,128)S(1)} fusion(f32[32,4,8,128]{3,2,1,0:T(8,128)S(1)} %bitcast.105, f32[32,4,128,128]{3,2,1,0:T(8,128)} %param.15), kind=kOutput, calls=%fused_computation.23 | convolution fusion | flops 201326592 | bytes 9043968 | tf_op jit(solution)/shard_map/blij,blmj->bmi/dot_general | solution.py:24
  71.1 9.3 %convolution_bitcast_fusion = f32[32,8,128]{2,1,0:T(8,128)S(1)} fusion(f32[32,4,8,128]{3,2,1,0:T(8,128)S(1)} %bitcast.103, f32[32,4,128,128]{3,2,1,0:T(8,128)} %param.15), kind=kOutput, calls=%fused_computation.21 | convolution fusion | flops 201326592 | bytes 9043968 | tf_op jit(solution)/shard_map/blij,blmj->bmi/dot_general | solution.py:24
  80.4 0.7 fusion.17
  81.2 0.7 fusion.15
  82.0 0.1 fusion.4
  82.2 0.1 fusion.13
  82.3 68.0 %gather_fusion = f32[12288]{0:T(1024)S(1)} fusion(f32[4096]{0:T(1024)S(1)} %fusion.13, s32[12288]{0:T(1024)S(1)} %broadcast_clamp_fusion), kind=kCustom, calls=%fused_computation.20 | custom fusion | bytes 147456 | tf_op jit(solution)/shard_map/jit(_take)/gather | solution.py:92
  150.5 44.1 %all-gather = f32[8192]{0:T(1024)S(1)} all-gather(f32[1024]{0:T(1024)S(1)} %broadcast_multiply_fusion.1), channel_id=2, replica_groups=mesh['freq'=8,'dom'=32] {'freq'}, dimensions={0}, use_global_device_ids=true | all-gather | bytes 36864 | tf_op jit(solution)/shard_map/all_gather | solution.py:95
  194.6 0.6 multiply_subtract_fusion
  (71 shorter events, 1.2 us)
Async XLA Ops:
  4.7 13.2 %collective-permute-start = (f32[16,8,128]{2,1,0:T(8,128)S(1)}, f32[16,8,128]{2,1,0:T(8,128)S(1)}, u32[]{:S(2)}, u32[]{:S(2)}) collective-permute-start(f32[16,8,128]{2,1,0:T(8,128)S(1)} %get-tuple-element.62), channel_id=1, source_target_pairs={{0,1},{1,0},{2,3},{3,2},{4,5},{5,4},{6,7},{7,6},{8,9},{9,8},{10,11... | collective-permute-start | bytes 196616 | tf_op jit(solution)/shard_map/ppermute | solution.py:12
  6.1 12.1 %collective-permute-start.1 = (f32[16,8,128]{2,1,0:T(8,128)S(1)}, f32[16,8,128]{2,1,0:T(8,128)S(1)}, u32[]{:S(2)}, u32[]{:S(2)}) collective-permute-start(f32[16,8,128]{2,1,0:T(8,128)S(1)} %get-tuple-element.60), channel_id=1, source_target_pairs={{0,2},{1,3},{2,0},{3,1},{4,6},{5,7},{6,4},{7,5},{8,10},{9,11},{10,... | collective-permute-start | bytes 196616 | tf_op jit(solution)/shard_map/ppermute | solution.py:12
  9.3 9.1 %collective-permute-start.2 = (f32[16,8,128]{2,1,0:T(8,128)S(1)}, f32[16,8,128]{2,1,0:T(8,128)S(1)}, u32[]{:S(2)}, u32[]{:S(2)}) collective-permute-start(f32[16,8,128]{2,1,0:T(8,128)S(1)} %get-tuple-element.58), channel_id=1, source_target_pairs={{0,4},{1,5},{2,6},{3,7},{4,0},{5,1},{6,2},{7,3},{8,12},{9,13},{10,... | collective-permute-start | bytes 196616 | tf_op jit(solution)/shard_map/ppermute | solution.py:12
  13.9 5.6 %collective-permute-start.3 = (f32[16,8,128]{2,1,0:T(8,128)S(1)}, f32[16,8,128]{2,1,0:T(8,128)S(1)}, u32[]{:S(2)}, u32[]{:S(2)}) collective-permute-start(f32[16,8,128]{2,1,0:T(8,128)S(1)} %get-tuple-element.56), channel_id=1, source_target_pairs={{0,8},{1,9},{2,10},{3,11},{4,12},{5,13},{6,14},{7,15},{8,0},{9,1},... | collective-permute-start | bytes 196616 | tf_op jit(solution)/shard_map/ppermute | solution.py:12
  15.2 5.1 %collective-permute-start.8 = (f32[16,8,128]{2,1,0:T(8,128)S(1)}, f32[16,8,128]{2,1,0:T(8,128)S(1)}, u32[]{:S(2)}, u32[]{:S(2)}) collective-permute-start(f32[16,8,128]{2,1,0:T(8,128)S(1)} %get-tuple-element.61), channel_id=1, source_target_pairs={{0,1},{1,0},{2,3},{3,2},{4,5},{5,4},{6,7},{7,6},{8,9},{9,8},{10,11... | collective-permute-start | bytes 196616 | tf_op jit(solution)/shard_map/ppermute | solution.py:12
  17.9 5.8 %collective-permute-start.9 = (f32[16,8,128]{2,1,0:T(8,128)S(1)}, f32[16,8,128]{2,1,0:T(8,128)S(1)}, u32[]{:S(2)}, u32[]{:S(2)}) collective-permute-start(f32[16,8,128]{2,1,0:T(8,128)S(1)} %get-tuple-element.59), channel_id=1, source_target_pairs={{0,2},{1,3},{2,0},{3,1},{4,6},{5,7},{6,4},{7,5},{8,10},{9,11},{10,... | collective-permute-start | bytes 196616 | tf_op jit(solution)/shard_map/ppermute | solution.py:12
  18.1 6.9 %collective-permute-start.10 = (f32[16,8,128]{2,1,0:T(8,128)S(1)}, f32[16,8,128]{2,1,0:T(8,128)S(1)}, u32[]{:S(2)}, u32[]{:S(2)}) collective-permute-start(f32[16,8,128]{2,1,0:T(8,128)S(1)} %get-tuple-element.57), channel_id=1, source_target_pairs={{0,4},{1,5},{2,6},{3,7},{4,0},{5,1},{6,2},{7,3},{8,12},{9,13},{10,... | collective-permute-start | bytes 196616 | tf_op jit(solution)/shard_map/ppermute | solution.py:12
  18.4 6.6 %collective-permute-start.11 = (f32[16,8,128]{2,1,0:T(8,128)S(1)}, f32[16,8,128]{2,1,0:T(8,128)S(1)}, u32[]{:S(2)}, u32[]{:S(2)}) collective-permute-start(f32[16,8,128]{2,1,0:T(8,128)S(1)} %get-tuple-element.55), channel_id=1, source_target_pairs={{0,8},{1,9},{2,10},{3,11},{4,12},{5,13},{6,14},{7,15},{8,0},{9,1},... | collective-permute-start | bytes 196616 | tf_op jit(solution)/shard_map/ppermute | solution.py:12
  26.0 18.7 %copy-start = (f32[2,4,32,128]{3,2,1,0:T(8,128)S(1)}, f32[2,4,32,128]{3,2,1,0:T(8,128)}, u32[]{:S(2)}) copy-start(f32[2,4,32,128]{3,2,1,0:T(8,128)} %param.14) | copy-start | bytes 393220
  26.0 18.7 %copy-start.1 = (f32[2,4,32,128]{3,2,1,0:T(8,128)S(1)}, f32[2,4,32,128]{3,2,1,0:T(8,128)}, u32[]{:S(2)}) copy-start(f32[2,4,32,128]{3,2,1,0:T(8,128)} %param.13) | copy-start | bytes 393220
  49.7 5.2 %collective-permute-start.4 = (f32[16,8,128]{2,1,0:T(8,128)S(1)}, f32[16,8,128]{2,1,0:T(8,128)S(1)}, u32[]{:S(2)}, u32[]{:S(2)}) collective-permute-start(f32[16,8,128]{2,1,0:T(8,128)S(1)} %get-tuple-element.52), channel_id=1, source_target_pairs={{0,1},{1,0},{2,3},{3,2},{4,5},{5,4},{6,7},{7,6},{8,9},{9,8},{10,11... | collective-permute-start | bytes 196616 | tf_op jit(solution)/shard_map/ppermute | solution.py:12
  49.9 5.8 %collective-permute-start.5 = (f32[16,8,128]{2,1,0:T(8,128)S(1)}, f32[16,8,128]{2,1,0:T(8,128)S(1)}, u32[]{:S(2)}, u32[]{:S(2)}) collective-permute-start(f32[16,8,128]{2,1,0:T(8,128)S(1)} %get-tuple-element.50), channel_id=1, source_target_pairs={{0,2},{1,3},{2,0},{3,1},{4,6},{5,7},{6,4},{7,5},{8,10},{9,11},{10,... | collective-permute-start | bytes 196616 | tf_op jit(solution)/shard_map/ppermute | solution.py:12
  50.4 7.0 %collective-permute-start.6 = (f32[16,8,128]{2,1,0:T(8,128)S(1)}, f32[16,8,128]{2,1,0:T(8,128)S(1)}, u32[]{:S(2)}, u32[]{:S(2)}) collective-permute-start(f32[16,8,128]{2,1,0:T(8,128)S(1)} %get-tuple-element.48), channel_id=1, source_target_pairs={{0,4},{1,5},{2,6},{3,7},{4,0},{5,1},{6,2},{7,3},{8,12},{9,13},{10,... | collective-permute-start | bytes 196616 | tf_op jit(solution)/shard_map/ppermute | solution.py:12
  52.8 4.9 %collective-permute-start.7 = (f32[16,8,128]{2,1,0:T(8,128)S(1)}, f32[16,8,128]{2,1,0:T(8,128)S(1)}, u32[]{:S(2)}, u32[]{:S(2)}) collective-permute-start(f32[16,8,128]{2,1,0:T(8,128)S(1)} %get-tuple-element.46), channel_id=1, source_target_pairs={{0,8},{1,9},{2,10},{3,11},{4,12},{5,13},{6,14},{7,15},{8,0},{9,1},... | collective-permute-start | bytes 196616 | tf_op jit(solution)/shard_map/ppermute | solution.py:12
  53.8 7.0 %collective-permute-start.15 = (f32[16,8,128]{2,1,0:T(8,128)S(1)}, f32[16,8,128]{2,1,0:T(8,128)S(1)}, u32[]{:S(2)}, u32[]{:S(2)}) collective-permute-start(f32[16,8,128]{2,1,0:T(8,128)S(1)} %get-tuple-element.45), channel_id=1, source_target_pairs={{0,8},{1,9},{2,10},{3,11},{4,12},{5,13},{6,14},{7,15},{8,0},{9,1},... | collective-permute-start | bytes 196616 | tf_op jit(solution)/shard_map/ppermute | solution.py:12
  55.0 5.8 %collective-permute-start.14 = (f32[16,8,128]{2,1,0:T(8,128)S(1)}, f32[16,8,128]{2,1,0:T(8,128)S(1)}, u32[]{:S(2)}, u32[]{:S(2)}) collective-permute-start(f32[16,8,128]{2,1,0:T(8,128)S(1)} %get-tuple-element.47), channel_id=1, source_target_pairs={{0,4},{1,5},{2,6},{3,7},{4,0},{5,1},{6,2},{7,3},{8,12},{9,13},{10,... | collective-permute-start | bytes 196616 | tf_op jit(solution)/shard_map/ppermute | solution.py:12
  55.7 5.1 %collective-permute-start.13 = (f32[16,8,128]{2,1,0:T(8,128)S(1)}, f32[16,8,128]{2,1,0:T(8,128)S(1)}, u32[]{:S(2)}, u32[]{:S(2)}) collective-permute-start(f32[16,8,128]{2,1,0:T(8,128)S(1)} %get-tuple-element.49), channel_id=1, source_target_pairs={{0,2},{1,3},{2,0},{3,1},{4,6},{5,7},{6,4},{7,5},{8,10},{9,11},{10,... | collective-permute-start | bytes 196616 | tf_op jit(solution)/shard_map/ppermute | solution.py:12
  57.4 1.6 collective-permute-start.12
  71.0 11.1 %copy-start.4 = (f32[2]{0:T(128)S(1)}, f32[2]{0:T(128)}, u32[]{:S(2)}) copy-start(f32[2]{0:T(128)} %param.19) | copy-start | bytes 28
  82.3 68.1 %copy-start.2 = (s32[12,1024]{1,0:T(8,128)S(1)}, s32[12,1024]{1,0:T(8,128)}, u32[]{:S(2)}) copy-start(s32[12,1024]{1,0:T(8,128)} %param.20) | copy-start | bytes 147460
  82.3 112.2 %copy-start.3 = (f32[1024]{0:T(1024)S(1)}, f32[1024]{0:T(1024)}, u32[]{:S(2)}) copy-start(f32[1024]{0:T(1024)} %param.21) | copy-start | bytes 12292
